TPU v7x, 256 devices: a whole 4x4x8 slice. The times are simulated.
256 devices in a mesh: pipe: 16 (over x, z_lo, core), tensor: 16 (over y, z_hi).
Axes of the slice: x: 4, y: 4, z: 8 (z_hi: 4, z_lo: 2; z = z_hi * 2 + z_lo), core: 2. Of those that a mesh axis runs over, the one named last changes fastest.
Arguments:
- hidden: bfloat16 [384, 8192], P('pipe', 'tensor'), may hold values from -64 to 64
- weight: bfloat16 [8192, 131072], P(None, ('pipe', 'tensor')), may hold values from -0.23201941 to 0.23201941
- targets: int32 [384], replicated, may hold values from 0 to 131071
- token_weight: float32 [384], replicated, may hold values from 0.1 to 1
Outputs:
- token_loss: float32 [384], P('pipe')
- hidden_grad: float32 [384, 8192], P('pipe', 'tensor')
All inputs are finite; a program needn't handle non-finite values.
Results may differ from a plain program's by a relative error of at most 0.0029.
Values may be sent and summed in bfloat16 or wider, within the bound.
No kernel may reach another device: no remote copies, remote signals or barrier semaphores. Data moves between devices by JAX's collectives and lax.ppermute only.
A program may use at most 128 MiB of HBM per device.

v0:
```python
import jax
import jax.numpy as jnp
from jax import lax
from jax.sharding import Mesh
from jax.sharding import PartitionSpec as P

TENSOR = ("tensor_0", "tensor_1")
PIPE = ("pipe_0", "pipe_1", "pipe_2")
PIPE_TENSOR = ("pipe_0", "pipe_1", "pipe_2", "tensor_0", "tensor_1")
loss_scale = 32.0


def sent_to_all(shard, axis):
    copies = jnp.broadcast_to(shard, (lax.axis_size(axis), *shard.shape))
    return lax.all_to_all(copies, axis, split_axis=0, concat_axis=0, tiled=True)


def joined_along(blocks, dim):
    blocks = jnp.moveaxis(blocks, 0, dim)
    lengths = blocks.shape
    return blocks.reshape(*lengths[:dim], lengths[dim] * lengths[dim + 1], *lengths[dim + 2 :])


def gather_directly(shard, axis, dim):
    blocks = sent_to_all(shard, axis)
    return joined_along(blocks, dim)


def all_in_one(shard, axis):
    leaves = jax.tree.leaves(shard)
    order = sorted(range(len(leaves)), key=lambda k: -leaves[k].size)
    width = (1, *leaves[order[0]].shape)[-1]
    lines = [
        jnp.pad(leaves[k].reshape(-1), (0, -leaves[k].size % width)).reshape(-1, width)
        for k in order
    ]
    both, at, found = (lax.all_gather(jnp.concatenate(lines), axis), 0, {})
    for k, line in zip(order, lines):
        piece = both[:, at : at + len(line)].reshape(len(both), -1)
        found[k] = piece[:, : leaves[k].size].reshape(-1, *leaves[k].shape)
        at += len(line)
    numbers = iter(range(len(leaves)))
    return jax.tree.map(lambda _: found[next(numbers)], shard)


def joined_all(shard, axes, combine):
    for axis in axes:
        pieces = all_in_one(shard, axis)
        shard = jax.tree.map(lambda part: part[0], pieces)
        for k in range(1, lax.axis_size(axis)):
            shard = combine(shard, jax.tree.map(lambda part: part[k], pieces))
    return shard


def cut_along(shard, dim, count):
    lengths = shard.shape
    blocks = shard.reshape(*lengths[:dim], count, lengths[dim] // count, *lengths[dim + 1 :])
    return jnp.moveaxis(blocks, dim, 0)


def sent_and_summed(shard, axis, dim):
    count = lax.axis_size(axis)
    blocks = lax.all_to_all(cut_along(shard, dim, count), axis, 0, 0, tiled=True)
    return jnp.sum(blocks, axis=0)


def combine_stats(left_stats, right_stats):
    left_peak, left_total, left_target = left_stats
    right_peak, right_total, right_target = right_stats
    joined = jnp.maximum(left_peak, right_peak)
    summed = left_total * jnp.exp(left_peak - joined) + right_total * jnp.exp(right_peak - joined)
    return (joined, summed, left_target + right_target)


def local(hidden, weight, targets, token_weight):
    rows_local = hidden.shape[0]
    width_local = weight.shape[1]
    full_rows = gather_directly(hidden, TENSOR, 1)
    logits = jnp.dot(
        lax.all_gather(full_rows, PIPE, axis=0, tiled=True),
        weight,
        preferred_element_type=jnp.float32,
    )
    device_block = lax.axis_index(PIPE) * lax.axis_size(TENSOR) + lax.axis_index(TENSOR)
    columns = device_block * width_local + jnp.arange(width_local, dtype=jnp.int32)
    target_hit = targets[:, None] == columns[None, :]
    chosen = jnp.sum(jnp.where(target_hit, logits, jnp.float32(0.0)), axis=1)
    local_peak = jnp.max(logits, axis=1)
    local_total = jnp.sum(jnp.exp(logits - local_peak[:, None]), axis=1)
    global_peak, global_total, target_logit = joined_all(
        (local_peak, local_total, chosen), PIPE_TENSOR, combine_stats
    )
    log_total = global_peak + jnp.log(global_total)
    loss_rows = log_total - target_logit
    token_loss = lax.dynamic_slice_in_dim(
        loss_rows, lax.axis_index(PIPE) * rows_local, rows_local, 0
    )
    softmax = jnp.exp(logits - log_total[:, None])
    dlogits = (
        loss_scale * token_weight[:, None] * (softmax - target_hit.astype(jnp.float32))
    ).astype(jnp.bfloat16)
    section_part = lax.psum_scatter(
        lax.dot_general(
            dlogits, weight, (((1,), (1,)), ((), ())), preferred_element_type=jnp.float32
        ),
        PIPE,
        scatter_dimension=0,
        tiled=True,
    )
    hidden_grad = sent_and_summed(section_part, TENSOR, 1)
    return (token_loss, hidden_grad)


def solution(mesh):
    split = Mesh(
        mesh.devices.reshape(4, 2, 2, 4, 4), ("pipe_0", "pipe_1", "pipe_2", "tensor_0", "tensor_1")
    )
    placed = (P(PIPE, TENSOR), P(None, PIPE_TENSOR), P(), P())
    return jax.shard_map(
        local, mesh=split, in_specs=placed, out_specs=(P(PIPE), P(PIPE, TENSOR)), check_vma=False
    )
```

profile of v0, /device:TPU:4, one launch (start us, length us, event | category | flops | bytes accessed | tf_op | source)
XLA Modules:
  0.0 324.7 jit_solution(18209849761081258595)
XLA Ops:
  7.2 0.0 all-gather.12.cloned.1.call-start
  7.2 0.8 broadcast_in_dim.6
  8.0 27.0 %all_to_all.10 = bf16[16,24,512]{2,1,0:T(8,128)(2,1)S(1)} all-to-all(bf16[16,24,512]{2,1,0:T(8,128)(2,1)S(1)} %broadcast_in_dim.6), channel_id=1, replica_groups=mesh['pipe_0'=4,'pipe_1'=2,'pipe_2'=2,'tensor_0'=4,'tensor_1'=4] {'tenso..., dimensions={0} | all-to-all | bytes 786432 | tf_op jit(solution)/shard_map/all_to_all | solution.py:15
  35.0 0.8 copy.9
  35.8 0.0 all-gather.12.cloned.1.call-update
  35.8 0.0 reduce-scatter.2.cloned.1.call-start
  35.9 0.7 broadcast_multiply_fusion
  36.6 0.0 copy-start
  36.6 38.5 %all-gather.12.cloned.1.call-done = bf16[384,8192]{1,0:T(8,128)(2,1)} async-done(((bf16[24,8192]{1,0:T(8,128)(2,1)}), bf16[384,8192]{1,0:T(8,128)(2,1)}) %all-gather.12.cloned.1.call-update) | async-done | bytes 6291472 | tf_op jit(solution)/shard_map/all_gather | solution.py:80
  75.1 8.0 %fusion.58 = (f32[384]{0:T(512)S(1)}, f32[384,512]{1,0:T(8,128)S(1)}) fusion(bf16[384,8192]{1,0:T(8,128)(2,1)} %all-gather.12.cloned.1.call-done, bf16[8192,512]{1,0:T(8,128)(2,1)} %param.5), kind=kOutput, calls=%fused_computation.111 | convolution fusion | flops 3221421568 | bytes 15468032 | tf_op jit(solution)/shard_map/dot_general | solution.py:79
  83.1 0.0 copy-done
  83.1 0.4 exponential_reduce_fusion
  83.5 11.0 %all-gather.5 = f32[4,3,384]{2,1,0:T(4,128)S(1)} all-gather(f32[1,3,384]{2,1,0:T(4,128)S(1)} %maximum_bitcast_fusion), channel_id=2, replica_groups=mesh['pipe_0'=4,'pipe_1'=2,'pipe_2'=2,'tensor_0'=4,'tensor_1'=4] {'pipe_0'}, dimensions={0}, use_global_device_ids=true | all-gather | bytes 23040 | tf_op jit(solution)/shard_map/all_gather | solution.py:37
  94.6 4.4 %all-gather.6 = f32[2,3,384]{2,1,0:T(4,128)S(1)} all-gather(f32[1,3,384]{2,1,0:T(4,128)S(1)} %maximum_bitcast_fusion.1), channel_id=3, replica_groups=mesh['pipe_0'=4,'pipe_1'=2,'pipe_2'=2,'tensor_0'=4,'tensor_1'=4] {'pipe_1'}, dimensions={0}, use_global_device_ids=true | all-gather | bytes 13824 | tf_op jit(solution)/shard_map/all_gather | solution.py:37
  99.1 1.8 all-gather.7
  100.9 12.3 %all-gather.8 = f32[4,3,384]{2,1,0:T(4,128)S(1)} all-gather(f32[1,3,384]{2,1,0:T(4,128)S(1)} %maximum_bitcast_fusion.3), channel_id=5, replica_groups=mesh['pipe_0'=4,'pipe_1'=2,'pipe_2'=2,'tensor_0'=4,'tensor_1'=4] {'tenso..., dimensions={0}, use_global_device_ids=true | all-gather | bytes 23040 | tf_op jit(solution)/shard_map/all_gather | solution.py:37
  113.3 15.7 %all-gather.9 = f32[4,3,384]{2,1,0:T(4,128)S(1)} all-gather(f32[1,3,384]{2,1,0:T(4,128)S(1)} %maximum_bitcast_fusion.4), channel_id=6, replica_groups=mesh['pipe_0'=4,'pipe_1'=2,'pipe_2'=2,'tensor_0'=4,'tensor_1'=4] {'tenso..., dimensions={0}, use_global_device_ids=true | all-gather | bytes 23040 | tf_op jit(solution)/shard_map/all_gather | solution.py:37
  129.0 0.1 fusion.16
  129.0 12.0 %fusion.4 = f32[384,8192]{1,0:T(8,128)} fusion(bf16[8192,512]{1,0:T(8,128)(2,1)} %param.5, f32[384,512]{1,0:T(8,128)S(1)} %get-tuple-element.24, f32[384]{0:T(512)S(1)} %get-tuple-element.14, f32[384]{0:T(512)S(1)} %broadcast_multiply_fusion, s32[512]{0:T(512)S(1)} %iota_add_fusion, s32[384]{0:T(512)S(1)} %copy-done), kind=kOutput, calls=%fused_computation.8 | convolution fusion | flops 3222405120 | bytes 21764608 | tf_op jit(solution)/shard_map/dot_general | solution.py:103
  141.1 0.0 reduce-scatter.2.cloned.1.call-update
  141.1 139.7 %reduce-scatter.2.cloned.1.call-done = f32[24,8192]{1,0:T(8,128)} async-done(((f32[384,8192]{1,0:T(8,128)}), f32[24,8192]{1,0:T(8,128)}) %reduce-scatter.2.cloned.1.call-update) | async-done | bytes 786448 | tf_op jit(solution)/shard_map/reduce_scatter | solution.py:102
  280.8 2.1 copy.11
  282.9 8.7 %all-to-all-start.1 = ((f32[16,24,512]{2,1,0:T(8,128)}), f32[16,24,512]{2,1,0:T(8,128)S(1)}, u32[]{:S(2)}, u32[]{:S(2)}) async-start(f32[16,24,512]{2,1,0:T(8,128)} %bitcast.226), calls=%async_computation.2 | async-start | bytes 1572864 | tf_op jit(solution)/shard_map/all_to_all | solution.py:63
  291.6 0.6 dynamic_slice.3
  292.2 25.0 %all-to-all-done.1 = f32[16,24,512]{2,1,0:T(8,128)S(1)} async-done(((f32[16,24,512]{2,1,0:T(8,128)}), f32[16,24,512]{2,1,0:T(8,128)S(1)}, u32[]{:S(2)}, u32[]{:S(2)}) %all-to-all-start.1) | async-done | bytes 786464 | tf_op jit(solution)/shard_map/all_to_all | solution.py:63
  317.2 0.7 reduce_sum.29
  (18 shorter events, 0.2 us)
Async XLA Ops:
  7.2 67.9 %all-gather.12.cloned.1.call-start = ((), (), s32[]{:S(2)}) async-start(), calls=%async_computation.3 | async-start | bytes 6684672 | tf_op jit(solution)/shard_map/all_gather | solution.py:80
  35.8 245.0 %reduce-scatter.2.cloned.1.call-start = ((), (), s32[]{:S(2)}) async-start(), calls=%async_computation.4 | async-start | bytes 13369344 | tf_op jit(solution)/shard_map/reduce_scatter | solution.py:102
  36.6 46.6 %copy-start = (s32[384]{0:T(512)S(1)}, s32[384]{0:T(512)}, u32[]{:S(2)}) copy-start(s32[384]{0:T(512)} %param.6) | copy-start | bytes 4612
  282.9 34.3 %all-to-all-start.1 = ((f32[16,24,512]{2,1,0:T(8,128)}), f32[16,24,512]{2,1,0:T(8,128)S(1)}, u32[]{:S(2)}, u32[]{:S(2)}) async-start(f32[16,24,512]{2,1,0:T(8,128)} %bitcast.226), calls=%async_computation.2 | async-start | bytes 1572864 | tf_op jit(solution)/shard_map/all_to_all | solution.py:63
Sparse Core Ops, SparseCore 0:
  35.9 39.1 all-gather.11
  141.2 139.5 reduce-scatter.1
where the time goes:
time: 325 us
  waiting for transfers between devices  203 us (62%)
  blocking collectives  72.2 us (22%)
  matrix products  20 us (6%)
  between operations  14.2 us (4%)
  starting transfers between devices  8.76 us (3%)
  local copies, waits for them, and re-layouts  4.22 us (1%)
    reduce_scatter x1, waiting for transfers between devices, local(): lax.psum_scatter(lax.dot_general(dlogits, weight, (((1,), (1,)), ((), ())...  140 us
    all_gather x5, blocking collectives, all_in_one(): both, at, found = (lax.all_gather(jnp.concatenate(lines), axis), 0, {})  45.2 us
    all_gather x1, waiting for transfers between devices, local(): lax.all_gather(full_rows, PIPE, axis=0, tiled=True)  38.5 us
    all_to_all x1, blocking collectives, sent_to_all(): return lax.all_to_all(copies, axis, split_axis=0, concat_axis=0, tiled=True)  27 us
    all_to_all x1, waiting for transfers between devices, sent_and_summed(): lax.all_to_all(cut_along(shard, dim, count), axis, 0, 0, tiled=True)  25 us
    dot_general x1, matrix products, local(): lax.dot_general(dlogits, weight, (((1,), (1,)), ((), ())), preferred_elem...  12 us
    all_to_all x1, starting transfers between devices, sent_and_summed(): lax.all_to_all(cut_along(shard, dim, count), axis, 0, 0, tiled=True)  8.68 us
    dot_general x1, matrix products, local(): jnp.dot(lax.all_gather(full_rows, PIPE, axis=0, tiled=True), weight, pref...  8 us
  transfers between devices with their start and end apart: 3, of which 3 were waited for; matrix products, arithmetic and copies ran while one was open for 0% of the time, Pallas kernels for 0%

commit v1 on v0

--- a/solution.py
+++ b/solution.py
@@ -77,7 +77,9 @@
     width_local = weight.shape[1]
     full_rows = gather_directly(hidden, TENSOR, 1)
     logits = jnp.dot(
-        lax.all_gather(full_rows, PIPE, axis=0, tiled=True),
+        jnp.concatenate(
+            lax.all_to_all(jnp.stack([full_rows] * lax.axis_size(PIPE)), PIPE, 0, 0), axis=0
+        ),
         weight,
         preferred_element_type=jnp.float32,
     )

time: 325 us -> 361 us (1.11)
  waiting for transfers between devices: 203 us -> 232 us
  starting transfers between devices: 8.76 us -> 14.1 us
    all_to_all x0 -> x1, waiting for transfers between devices: none -> 70.2 us  [local(): lax.all_to_all(jnp.stack([full_rows] * lax.axis_size(PIPE)), PIPE, 0, 0)]
    all_gather x1 -> x0, waiting for transfers between devices: 38.5 us -> none  [local(): lax.all_gather(full_rows, PIPE, axis=0, tiled=True)]
    all_to_all x0 -> x1, starting transfers between devices: none -> 5.44 us  [local(): lax.all_to_all(jnp.stack([full_rows] * lax.axis_size(PIPE)), PIPE, 0, 0)]
where the time goes in v1:
time: 361 us; the launch traced here: 360 us
  waiting for transfers between devices  232 us (64%)
  blocking collectives  71.5 us (20%)
  matrix products  20 us (6%)
  between operations  14.2 us (4%)
  starting transfers between devices  14.1 us (4%)
  local copies, waits for them, and re-layouts  6.85 us (2%)
    reduce_scatter x1, waiting for transfers between devices, local(): lax.psum_scatter(lax.dot_general(dlogits, weight, (((1,), (1,)), ((), ())...  137 us
    all_to_all x1, waiting for transfers between devices, local(): lax.all_to_all(jnp.stack([full_rows] * lax.axis_size(PIPE)), PIPE, 0, 0)  70.2 us
    all_gather x5, blocking collectives, all_in_one(): both, at, found = (lax.all_gather(jnp.concatenate(lines), axis), 0, {})  44.5 us
    all_to_all x1, blocking collectives, sent_to_all(): return lax.all_to_all(copies, axis, split_axis=0, concat_axis=0, tiled=True)  27 us
    all_to_all x1, waiting for transfers between devices, sent_and_summed(): lax.all_to_all(cut_along(shard, dim, count), axis, 0, 0, tiled=True)  25 us
    dot_general x1, matrix products, local(): lax.dot_general(dlogits, weight, (((1,), (1,)), ((), ())), preferred_elem...  12 us
    all_to_all x1, starting transfers between devices, sent_and_summed(): lax.all_to_all(cut_along(shard, dim, count), axis, 0, 0, tiled=True)  8.66 us
    dot_general x1, matrix products, local(): jnp.dot(jnp.concatenate(lax.all_to_all(jnp.stack([full_rows] * lax.axis_s...  8.02 us
  transfers between devices with their start and end apart: 3, of which 3 were waited for; matrix products, arithmetic and copies ran while one was open for 0% of the time, Pallas kernels for 0%

profile of v1, /device:TPU:4, one launch (start us, length us, event | category | flops | bytes accessed | tf_op | source)
XLA Modules:
  0.0 360.4 jit_solution(11353937692345249856)
XLA Ops:
  7.2 0.8 broadcast_in_dim.6
  7.9 27.0 %all_to_all.15 = bf16[16,24,512]{2,1,0:T(8,128)(2,1)S(1)} all-to-all(bf16[16,24,512]{2,1,0:T(8,128)(2,1)S(1)} %broadcast_in_dim.6), channel_id=1, replica_groups=mesh['pipe_0'=4,'pipe_1'=2,'pipe_2'=2,'tensor_0'=4,'tensor_1'=4] {'tenso..., dimensions={0} | all-to-all | bytes 786432 | tf_op jit(solution)/shard_map/all_to_all | solution.py:15
  35.0 3.4 stack.3
  38.4 5.4 %all-to-all-start.1 = ((bf16[16,24,8192]{2,1,0:T(8,128)(2,1)}), bf16[16,24,8192]{2,1,0:T(8,128)(2,1)}, u32[]{:S(2)}, u32[]{:S(2)}) async-start(bf16[16,24,8192]{2,1,0:T(8,128)(2,1)} %stack.3), calls=%async_computation.1 | async-start | bytes 12582912 | tf_op jit(solution)/shard_map/all_to_all | solution.py:81
  43.8 0.0 reduce-scatter.2.cloned.1.call-start
  43.9 70.2 %all-to-all-done.1 = bf16[16,24,8192]{2,1,0:T(8,128)(2,1)} async-done(((bf16[16,24,8192]{2,1,0:T(8,128)(2,1)}), bf16[16,24,8192]{2,1,0:T(8,128)(2,1)}, u32[]{:S(2)}, u32[]{:S(2)}) %all-to-all-start.1) | async-done | bytes 6291488 | tf_op jit(solution)/shard_map/all_to_all | solution.py:81
  114.1 0.0 copy-start
  114.1 0.0 copy-start.1
  114.1 8.0 %fusion.58 = (f32[384]{0:T(512)S(1)}, f32[384,512]{1,0:T(8,128)S(1)}) fusion(bf16[384,8192]{1,0:T(8,128)(2,1)} %bitcast.1, bf16[8192,512]{1,0:T(8,128)(2,1)} %param.5), kind=kOutput, calls=%fused_computation.111 | convolution fusion | flops 3221421568 | bytes 15468032 | tf_op jit(solution)/shard_map/dot_general | solution.py:79
  122.1 0.0 copy-done
  122.1 0.4 exponential_reduce_fusion
  122.5 12.6 %all-gather.5 = f32[4,3,384]{2,1,0:T(4,128)S(1)} all-gather(f32[1,3,384]{2,1,0:T(4,128)S(1)} %maximum_bitcast_fusion), channel_id=2, replica_groups=mesh['pipe_0'=4,'pipe_1'=2,'pipe_2'=2,'tensor_0'=4,'tensor_1'=4] {'pipe_0'}, dimensions={0}, use_global_device_ids=true | all-gather | bytes 23040 | tf_op jit(solution)/shard_map/all_gather | solution.py:37
  135.2 4.4 %all-gather.6 = f32[2,3,384]{2,1,0:T(4,128)S(1)} all-gather(f32[1,3,384]{2,1,0:T(4,128)S(1)} %maximum_bitcast_fusion.1), channel_id=3, replica_groups=mesh['pipe_0'=4,'pipe_1'=2,'pipe_2'=2,'tensor_0'=4,'tensor_1'=4] {'pipe_1'}, dimensions={0}, use_global_device_ids=true | all-gather | bytes 13824 | tf_op jit(solution)/shard_map/all_gather | solution.py:37
  139.6 1.8 all-gather.7
  141.5 12.0 %all-gather.8 = f32[4,3,384]{2,1,0:T(4,128)S(1)} all-gather(f32[1,3,384]{2,1,0:T(4,128)S(1)} %maximum_bitcast_fusion.3), channel_id=5, replica_groups=mesh['pipe_0'=4,'pipe_1'=2,'pipe_2'=2,'tensor_0'=4,'tensor_1'=4] {'tenso..., dimensions={0}, use_global_device_ids=true | all-gather | bytes 23040 | tf_op jit(solution)/shard_map/all_gather | solution.py:37
  153.5 13.8 %all-gather.9 = f32[4,3,384]{2,1,0:T(4,128)S(1)} all-gather(f32[1,3,384]{2,1,0:T(4,128)S(1)} %maximum_bitcast_fusion.4), channel_id=6, replica_groups=mesh['pipe_0'=4,'pipe_1'=2,'pipe_2'=2,'tensor_0'=4,'tensor_1'=4] {'tenso..., dimensions={0}, use_global_device_ids=true | all-gather | bytes 23040 | tf_op jit(solution)/shard_map/all_gather | solution.py:37
  167.3 0.1 fusion.16
  167.3 0.0 copy-done.1
  167.4 12.0 %fusion.4 = f32[384,8192]{1,0:T(8,128)} fusion(bf16[8192,512]{1,0:T(8,128)(2,1)} %param.5, f32[384,512]{1,0:T(8,128)S(1)} %get-tuple-element.24, f32[384]{0:T(512)S(1)} %get-tuple-element.14, f32[384]{0:T(512)S(1)} %get-tuple-element.25, s32[512]{0:T(512)S(1)} %iota_add_fusion, s32[384]{0:T(512)S(1)} %copy-done), kind=kOutput, calls=%fused_computation.8 | convolution fusion | flops 3222405120 | bytes 21764608 | tf_op jit(solution)/shard_map/dot_general | solution.py:105
  179.4 0.0 reduce-scatter.2.cloned.1.call-update
  179.4 137.1 %reduce-scatter.2.cloned.1.call-done = f32[24,8192]{1,0:T(8,128)} async-done(((f32[384,8192]{1,0:T(8,128)}), f32[24,8192]{1,0:T(8,128)}) %reduce-scatter.2.cloned.1.call-update) | async-done | bytes 786448 | tf_op jit(solution)/shard_map/reduce_scatter | solution.py:104
  316.5 2.1 copy.11
  318.5 8.7 %all-to-all-start.2 = ((f32[16,24,512]{2,1,0:T(8,128)}), f32[16,24,512]{2,1,0:T(8,128)S(1)}, u32[]{:S(2)}, u32[]{:S(2)}) async-start(f32[16,24,512]{2,1,0:T(8,128)} %bitcast.227), calls=%async_computation.3 | async-start | bytes 1572864 | tf_op jit(solution)/shard_map/all_to_all | solution.py:63
  327.2 0.6 dynamic_slice.3
  327.8 25.0 %all-to-all-done.2 = f32[16,24,512]{2,1,0:T(8,128)S(1)} async-done(((f32[16,24,512]{2,1,0:T(8,128)}), f32[16,24,512]{2,1,0:T(8,128)S(1)}, u32[]{:S(2)}, u32[]{:S(2)}) %all-to-all-start.2) | async-done | bytes 786464 | tf_op jit(solution)/shard_map/all_to_all | solution.py:63
  352.8 0.7 reduce_sum.29
  (19 shorter events, 0.2 us)
Async XLA Ops:
  38.4 75.7 %all-to-all-start.1 = ((bf16[16,24,8192]{2,1,0:T(8,128)(2,1)}), bf16[16,24,8192]{2,1,0:T(8,128)(2,1)}, u32[]{:S(2)}, u32[]{:S(2)}) async-start(bf16[16,24,8192]{2,1,0:T(8,128)(2,1)} %stack.3), calls=%async_computation.1 | async-start | bytes 12582912 | tf_op jit(solution)/shard_map/all_to_all | solution.py:81
  43.8 272.7 %reduce-scatter.2.cloned.1.call-start = ((), (), s32[]{:S(2)}) async-start(), calls=%async_computation.4 | async-start | bytes 13369344 | tf_op jit(solution)/shard_map/reduce_scatter | solution.py:104
  114.1 8.0 %copy-start = (s32[384]{0:T(512)S(1)}, s32[384]{0:T(512)}, u32[]{:S(2)}) copy-start(s32[384]{0:T(512)} %param.6) | copy-start | bytes 4612
  114.1 53.2 %copy-start.1 = (f32[384]{0:T(512)S(1)}, f32[384]{0:T(512)}, u32[]{:S(2)}) copy-start(f32[384]{0:T(512)} %param.7) | copy-start | bytes 4612
  318.5 34.3 %all-to-all-start.2 = ((f32[16,24,512]{2,1,0:T(8,128)}), f32[16,24,512]{2,1,0:T(8,128)S(1)}, u32[]{:S(2)}, u32[]{:S(2)}) async-start(f32[16,24,512]{2,1,0:T(8,128)} %bitcast.227), calls=%async_computation.3 | async-start | bytes 1572864 | tf_op jit(solution)/shard_map/all_to_all | solution.py:63
Sparse Core Ops, SparseCore 0:
  179.5 136.9 reduce-scatter.1
